TPU v7x, 256 devices: a whole 4x4x8 slice. The times are simulated.
256 devices in a mesh: dp: 2 (over x_lo), expert: 8 (over z), shard: 16 (over x_hi, y, core).
Axes of the slice: x: 4 (x_hi: 2, x_lo: 2; x = x_hi * 2 + x_lo), y: 4, z: 8, core: 2. Of those that a mesh axis runs over, the one named last changes fastest.
Arguments:
- tokens: bfloat16 [2048, 6144], P(('dp', 'expert', 'shard')), may hold values from -6 to 6
- gate_up_weight: bfloat16 [8, 2, 8192, 6144], P(None, None, ('dp', 'expert', 'shard')), may hold values from -0.078125 to 0.078125
- down_weight: bfloat16 [8, 8192, 6144], P(None, ('dp', 'expert', 'shard')), may hold values from -0.0625 to 0.0625
- expert_ids: int32 [2048, 2], P(('dp', 'expert', 'shard')), may hold values from 0 to 7, as said below
- slot_ids: int32 [2048, 2], P(('dp', 'expert', 'shard')), may hold values from 0 to 3, as said below
- gate_values: float32 [2048, 2], P(('dp', 'expert', 'shard')), may hold values from 0.1 to 1
- old_place: int32 [8], replicated, may hold values from 0 to 7, each once
- new_place: int32 [8], replicated, may hold values from 0 to 7, each once
Outputs:
- mixed_out: bfloat16 [2048, 6144], P(('dp', 'expert', 'shard'))
Inputs may be any that keep to these rules, and one draw needn't show every extreme that they name: `expert_ids`: each token names 2 different experts; among the 8 tokens of one block no expert is named more than 4 times, and one expert is named exactly 4 times in every block. `slot_ids`: within one block, two choices that name the same expert have different slots. `old_place`: each expert number appears once. `new_place`: each expert number appears once.
All inputs are finite; a program needn't handle non-finite values.
Results may differ from a plain program's by a relative error of at most 0.02.
Values may be sent and summed in bfloat16 or wider, within the bound.
A program may use at most 128 MiB of HBM per device.

v0:
```python
import jax
import jax.numpy as jnp
from jax import lax
from jax.sharding import PartitionSpec as P


def placement_order(old_place, new_place):
    slot_total = old_place.shape[0]
    matches = (new_place[:, None] == old_place[None, :]).astype(jnp.int32)
    return jnp.sum(matches * jnp.arange(slot_total, dtype=jnp.int32)[None, :], axis=1)


def swiglu_rows(row_block, pair_weight):
    gate_up = jnp.einsum("rd,gud->rgu", row_block, pair_weight, preferred_element_type=jnp.float32)
    return (jax.nn.silu(gate_up[:, 0]) * gate_up[:, 1]).astype(jnp.bfloat16)


def local(
    tokens, gate_up_weight, down_weight, expert_ids, slot_ids, gate_values, old_place, new_place
):
    experts = gate_up_weight.shape[0]
    sliver = gate_up_weight.shape[2]
    model_width = tokens.shape[1]
    tok_rows = tokens.shape[0]
    choices_per_token = expert_ids.shape[1]
    capacity = 2 * tok_rows * choices_per_token // experts
    cell_count = experts * capacity
    data_ways = lax.axis_size("dp")
    slot_order = placement_order(old_place, new_place)
    cell_ids = expert_ids * capacity + slot_ids
    cell_range = jnp.arange(cell_count, dtype=jnp.int32)
    cell_hits = (cell_ids[:, :, None] == cell_range[None, None, :]).astype(jnp.float32)
    token_picks = jnp.sum(cell_hits, axis=1)
    dispatched = jnp.dot(
        token_picks.T.astype(jnp.bfloat16), tokens, preferred_element_type=jnp.float32
    ).astype(jnp.bfloat16)
    received = lax.all_to_all(
        dispatched.reshape(experts, capacity, model_width),
        "expert",
        split_axis=0,
        concat_axis=0,
        tiled=True,
    )
    own_rows = received.reshape(cell_count, model_width)
    sectioned_in = gate_up_weight.reshape(experts, 2, data_ways, sliver // data_ways, model_width)
    sectioned_down = down_weight.reshape(experts, 1, data_ways, sliver // data_ways, model_width)
    sectioned_in = jnp.take(sectioned_in, slot_order, axis=0)
    sectioned_down = jnp.take(sectioned_down, slot_order, axis=0)
    relaid_in, relaid_down = (
        lax.all_to_all(
            lax.all_to_all(sectioned_in, "dp", split_axis=2, concat_axis=3, tiled=True),
            "expert",
            split_axis=0,
            concat_axis=3,
            tiled=True,
        ),
        lax.all_to_all(
            lax.all_to_all(sectioned_down, "dp", split_axis=2, concat_axis=3, tiled=True),
            "expert",
            split_axis=0,
            concat_axis=3,
            tiled=True,
        ),
    )
    full_in, full_down = (
        lax.all_gather(relaid_in, "dp", axis=3, tiled=True),
        lax.all_gather(relaid_down, "dp", axis=3, tiled=True),
    )
    pair_in = full_in.reshape(2, -1, model_width)
    pair_down = full_down.reshape(-1, model_width)
    group_rows = lax.all_gather(own_rows, "shard", axis=0, tiled=True)
    summed = lax.psum_scatter(
        jnp.dot(
            swiglu_rows(group_rows, pair_in), pair_down, preferred_element_type=jnp.float32
        ).astype(jnp.bfloat16),
        "shard",
        scatter_dimension=0,
        tiled=True,
    )
    returned = lax.all_to_all(
        summed.reshape(experts, capacity, model_width),
        "expert",
        split_axis=0,
        concat_axis=0,
        tiled=True,
    )
    combine_weights = jnp.sum(cell_hits * gate_values[:, :, None], axis=1)
    mixed_out = jnp.dot(
        combine_weights,
        returned.reshape(cell_count, model_width).astype(jnp.float32),
        precision=lax.Precision.HIGHEST,
    )
    return mixed_out.astype(jnp.bfloat16)


def solution(mesh):
    in_specs = (
        P(("dp", "expert", "shard"), None),
        P(None, None, ("dp", "expert", "shard"), None),
        P(None, ("dp", "expert", "shard"), None),
        P(("dp", "expert", "shard"), None),
        P(("dp", "expert", "shard"), None),
        P(("dp", "expert", "shard"), None),
        P(),
        P(),
    )
    out_specs = P(("dp", "expert", "shard"), None)
    return jax.shard_map(local, mesh=mesh, in_specs=in_specs, out_specs=out_specs, check_vma=False)
```

profile of v0, /device:TPU:8, one launch (start us, length us, event | category | flops | bytes accessed | tf_op | source)
XLA Modules:
  0.0 681.6 jit_solution(10519561180992360223)
XLA Ops:
  6.5 0.0 copy-start
  6.5 0.8 multiply_add_fusion
  7.4 0.9 convert_reduce_fusion
  8.3 1.2 convolution_convert_fusion.1
  9.5 0.9 reshape.64
  10.4 8.5 %all-to-all-start = ((bf16[8,4,6144]{2,1,0:T(4,128)(2,1)}), bf16[8,4,6144]{2,1,0:T(4,128)(2,1)S(1)}, u32[]{:S(2)}, u32[]{:S(2)}) async-start(bf16[8,4,6144]{2,1,0:T(4,128)(2,1)} %reshape.64), calls=%async_computation | async-start | bytes 786432 | tf_op jit(solution)/shard_map/all_to_all | solution.py:37
  18.8 0.9 select_reduce_fusion.1
  19.7 6.4 gather_fusion
  26.1 3.5 broadcast_select_fusion
  29.6 3.1 copy.24
  32.6 0.9 all-to-all-done
  33.5 6.3 all-to-all-start.1
  39.8 0.0 all-gather.4.cloned.1.call-start
  39.9 0.9 reshape.65
  40.7 0.0 all-gather.4.cloned.1.call-update
  40.8 0.0 all-gather.6.cloned.1.call-start
  40.8 89.5 %all-to-all-done.1 = bf16[8,2,2,16,6144]{4,3,1,0,2:T(8,128)(2,1)} async-done(((bf16[8,2,2,16,6144]{4,3,1,0,2:T(8,128)(2,1)}), bf16[8,2,2,16,6144]{4,3,1,0,2:T(8,128)(2,1)}, u32[]{:S(2)}, u32[]{:S(2)}) %all-to-all-start.1) | async-done | bytes 6291488 | tf_op jit(solution)/shard_map/all_to_all | solution.py:51
  130.3 3.5 copy.25
  133.8 145.8 %all_to_all.64 = bf16[8,2,1,32,6144]{4,3,1,2,0:T(8,128)(2,1)S(1)} all-to-all(bf16[8,2,1,32,6144]{4,3,1,2,0:T(8,128)(2,1)S(1)} %bitcast.37), channel_id=1, replica_groups=mesh['dp'=2,'expert'=8,'shard'=16] {'expert'}, dimensions={0} | all-to-all | bytes 12582912 | tf_op jit(solution)/shard_map/all_to_all | solution.py:50
  279.7 3.1 copy.27
  282.8 0.0 all-gather.6.cloned.1.call-update
  282.8 0.0 all-gather.8.cloned.1.call-start
  282.8 0.0 copy-done
  282.8 2.4 gather_fusion.1
  285.3 2.3 bitcast_select_fusion
  287.5 0.3 copy.28
  287.9 63.1 %all_to_all.65 = bf16[8,1,2,16,6144]{4,3,0,1,2:T(8,128)(2,1)S(1)} all-to-all(bf16[8,1,2,16,6144]{4,3,0,1,2:T(8,128)(2,1)S(1)} %copy.28), channel_id=1, replica_groups=mesh['dp'=2,'expert'=8,'shard'=16] {'dp'}, dimensions={2} | all-to-all | bytes 6291456 | tf_op jit(solution)/shard_map/all_to_all | solution.py:58
  350.9 0.3 copy.29
  351.2 66.1 %all_to_all.66 = bf16[8,1,1,32,6144]{4,3,2,1,0:T(8,128)(2,1)} all-to-all(bf16[8,1,1,32,6144]{4,3,2,1,0:T(8,128)(2,1)S(1)} %bitcast.40), channel_id=1, replica_groups=mesh['dp'=2,'expert'=8,'shard'=16] {'expert'}, dimensions={0} | all-to-all | bytes 6291456 | tf_op jit(solution)/shard_map/all_to_all | solution.py:57
  417.4 0.0 all-gather.8.cloned.1.call-update
  417.4 0.0 reduce-scatter.2.cloned.1.call-start
  417.5 0.0 all-gather.4.cloned.1.call-done
  417.5 41.2 %all-gather.6.cloned.1.call-done = bf16[1,2,1,512,6144]{4,3,1,2,0:T(8,128)(2,1)} async-done(((bf16[1,2,1,256,6144]{4,3,1,2,0:T(8,128)(2,1)}), bf16[1,2,1,512,6144]{4,3,1,2,0:T(8,128)(2,1)}) %all-gather.6.cloned.1.call-update) | async-done | bytes 12582928 | tf_op jit(solution)/shard_map/all_gather | solution.py:66
  458.6 12.5 %fusion = f32[512,2,512]{2,0,1:T(8,128)} fusion(bf16[1,2,1,512,6144]{4,3,1,2,0:T(8,128)(2,1)} %all-gather.6.cloned.1.call-done, bf16[512,6144]{1,0:T(8,128)(2,1)} %all-gather.4.cloned.1.call-done), kind=kOutput, calls=%fused_computation.2 | convolution fusion | flops 6442450944 | bytes 20971520 | tf_op jit(solution)/shard_map/rd,gud->rgu/dot_general | solution.py:14
  471.2 72.6 %all-gather.8.cloned.1.call-done = bf16[1,1,1,512,6144]{4,3,2,1,0:T(8,128)(2,1)} async-done(((bf16[1,1,1,256,6144]{4,3,2,1,0:T(8,128)(2,1)}), bf16[1,1,1,512,6144]{4,3,2,1,0:T(8,128)(2,1)}) %all-gather.8.cloned.1.call-update) | async-done | bytes 6291472 | tf_op jit(solution)/shard_map/all_gather | solution.py:67
  543.8 0.0 copy-start.1
  543.8 9.7 %convolution_convert_fusion = bf16[512,6144]{1,0:T(8,128)(2,1)} fusion(bf16[1,1,1,512,6144]{4,3,2,1,0:T(8,128)(2,1)} %all-gather.8.cloned.1.call-done, f32[512,2,512]{2,0,1:T(8,128)} %fusion), kind=kOutput, calls=%fused_computation.4 | convolution fusion | flops 3225944064 | bytes 14680064 | tf_op jit(solution)/shard_map/dot_general | solution.py:73
  553.5 0.0 reduce-scatter.2.cloned.1.call-update
  553.6 98.3 %reduce-scatter.2.cloned.1.call-done = bf16[32,6144]{1,0:T(8,128)(2,1)} async-done(((bf16[512,6144]{1,0:T(8,128)(2,1)}), bf16[32,6144]{1,0:T(8,128)(2,1)}) %reduce-scatter.2.cloned.1.call-update) | async-done | bytes 393232 | tf_op jit(solution)/shard_map/reduce_scatter | solution.py:72
  651.9 1.1 reshape.70
  653.0 20.0 %all_to_all.67 = bf16[8,4,6144]{2,1,0:T(4,128)(2,1)} all-to-all(bf16[8,4,6144]{2,1,0:T(4,128)(2,1)S(1)} %reshape.70), channel_id=1, replica_groups=mesh['dp'=2,'expert'=8,'shard'=16] {'expert'}, dimensions={0} | all-to-all | bytes 786432 | tf_op jit(solution)/shard_map/all_to_all | solution.py:80
  673.1 1.1 reshape.71
  674.1 0.9 convolution_convert_fusion.2
  675.1 0.0 copy-done.1
  (3 shorter events, 0.0 us)
Async XLA Ops:
  6.5 276.3 %copy-start = (bf16[8,32,6144]{2,1,0:T(8,128)(2,1)S(1)}, bf16[8,32,6144]{2,1,0:T(8,128)(2,1)}, u32[]{:S(2)}) copy-start(bf16[8,32,6144]{2,1,0:T(8,128)(2,1)} %param.10) | copy-start | bytes 9437188
  10.4 23.2 %all-to-all-start = ((bf16[8,4,6144]{2,1,0:T(4,128)(2,1)}), bf16[8,4,6144]{2,1,0:T(4,128)(2,1)S(1)}, u32[]{:S(2)}, u32[]{:S(2)}) async-start(bf16[8,4,6144]{2,1,0:T(4,128)(2,1)} %reshape.64), calls=%async_computation | async-start | bytes 786432 | tf_op jit(solution)/shard_map/all_to_all | solution.py:37
  33.5 96.8 %all-to-all-start.1 = ((bf16[8,2,2,16,6144]{4,3,1,0,2:T(8,128)(2,1)}), bf16[8,2,2,16,6144]{4,3,1,0,2:T(8,128)(2,1)}, u32[]{:S(2)}, u32[]{:S(2)}) async-start(bf16[8,2,2,16,6144]{4,3,1,0,2:T(8,128)(2,1)} %copy.24), calls=%async_computation.1 | async-start | bytes 12582912 | tf_op jit(solution)/shard_map/all_to_all | solution.py:51
  39.8 377.6 %all-gather.4.cloned.1.call-start = ((), (), s32[]{:S(2)}) async-start(), calls=%async_computation.7 | async-start | bytes 6684672 | tf_op jit(solution)/shard_map/all_gather | solution.py:71
  40.8 417.9 %all-gather.6.cloned.1.call-start = ((), (), s32[]{:S(2)}) async-start(), calls=%async_computation.8 | async-start | bytes 18874368 | tf_op jit(solution)/shard_map/all_gather | solution.py:66
  282.8 261.0 %all-gather.8.cloned.1.call-start = ((), (), s32[]{:S(2)}) async-start(), calls=%async_computation.9 | async-start | bytes 9437184 | tf_op jit(solution)/shard_map/all_gather | solution.py:67
  417.4 234.5 %reduce-scatter.2.cloned.1.call-start = ((), (), s32[]{:S(2)}) async-start(), calls=%async_computation.10 | async-start | bytes 6684672 | tf_op jit(solution)/shard_map/reduce_scatter | solution.py:72
  543.8 131.2 %copy-start.1 = (bf16[8,32,6144]{2,1,0:T(8,128)(2,1)S(1)}, bf16[8,32,6144]{2,1,0:T(8,128)(2,1)}, u32[]{:S(2)}) copy-start(bf16[8,32,6144]{2,1,0:T(8,128)(2,1)} %param.10) | copy-start | bytes 9437188
Sparse Core Ops, SparseCore 0:
  43.4 90.1 all-gather.3
  282.9 175.6 all-gather.5
  460.4 83.3 all-gather.7
  553.7 98.1 reduce-scatter.1
where the time goes:
time: 682 us
  waiting for transfers between devices  303 us (44%)
  blocking collectives  295 us (43%)
  matrix products  24.3 us (4%)
  local copies, waits for them, and re-layouts  23.1 us (3%)
  starting transfers between devices  15 us (2%)
  between operations  13.2 us (2%)
  other arithmetic  8.31 us (1%)
    all_to_all x1, blocking collectives, local(): lax.all_to_all(lax.all_to_all(sectioned_in, 'dp', split_axis=2, concat_ax...  146 us
    reduce_scatter x1, waiting for transfers between devices, local(): lax.psum_scatter(jnp.dot(swiglu_rows(group_rows, pair_in), pair_down, pre...  98.3 us
    all_to_all x1, waiting for transfers between devices, local(): lax.all_to_all(sectioned_in, 'dp', split_axis=2, concat_axis=3, tiled=True)  89.5 us
    all_gather x1, waiting for transfers between devices, local(): lax.all_gather(relaid_down, 'dp', axis=3, tiled=True)  72.6 us
    all_to_all x1, blocking collectives, local(): lax.all_to_all(lax.all_to_all(sectioned_down, 'dp', split_axis=2, concat_...  66.1 us
    all_to_all x1, blocking collectives, local(): lax.all_to_all(sectioned_down, 'dp', split_axis=2, concat_axis=3, tiled=T...  63.1 us
    all_gather x1, waiting for transfers between devices, local(): lax.all_gather(relaid_in, 'dp', axis=3, tiled=True)  41.2 us
    all_to_all x1, blocking collectives, local(): lax.all_to_all(summed.reshape(experts, capacity, model_width), 'expert',...  20 us
  transfers between devices with their start and end apart: 6, of which 5 were waited for; matrix products, arithmetic and copies ran while one was open for 6% of the time, Pallas kernels for 0%

commit v1 on v0

--- a/solution.py
+++ b/solution.py
@@ -2,6 +2,13 @@
 import jax.numpy as jnp
 from jax import lax
 from jax.sharding import PartitionSpec as P
+
+
+def exchange_gather(shard, name, along):
+    n_dev = lax.axis_size(name)
+    blocks = jnp.stack([shard for _ in range(n_dev)])
+    blocks = lax.all_to_all(blocks, name, split_axis=0, concat_axis=0)
+    return jnp.concatenate(blocks, axis=along)
 
 
 def placement_order(old_place, new_place):
@@ -64,7 +71,7 @@
     )
     full_in, full_down = (
         lax.all_gather(relaid_in, "dp", axis=3, tiled=True),
-        lax.all_gather(relaid_down, "dp", axis=3, tiled=True),
+        exchange_gather(relaid_down, "dp", 3),
     )
     pair_in = full_in.reshape(2, -1, model_width)
     pair_down = full_down.reshape(-1, model_width)

time: 682 us -> 661 us (0.969)
  waiting for transfers between devices: 303 us -> 272 us
    all_gather x1 -> x0, waiting for transfers between devices: 72.6 us -> none  [local(): lax.all_gather(relaid_down, 'dp', axis=3, tiled=True)]
    all_gather x1, waiting for transfers between devices: 41.2 us -> 68.2 us  [local(): lax.all_gather(relaid_in, 'dp', axis=3, tiled=True)]
    all_to_all x0 -> x1, waiting for transfers between devices: none -> 18.4 us  [exchange_gather(): blocks = lax.all_to_all(blocks, name, split_axis=0, concat_axis=0)]
where the time goes in v1:
time: 661 us
  blocking collectives  295 us (45%)
  waiting for transfers between devices  272 us (41%)
  matrix products  24.3 us (4%)
  local copies, waits for them, and re-layouts  23.1 us (3%)
  starting transfers between devices  21.2 us (3%)
  between operations  13.2 us (2%)
  other arithmetic  11.5 us (2%)
    all_to_all x1, blocking collectives, local(): lax.all_to_all(lax.all_to_all(sectioned_in, 'dp', split_axis=2, concat_ax...  146 us
    reduce_scatter x1, waiting for transfers between devices, local(): lax.psum_scatter(jnp.dot(swiglu_rows(group_rows, pair_in), pair_down, pre...  95.3 us
    all_to_all x1, waiting for transfers between devices, local(): lax.all_to_all(sectioned_in, 'dp', split_axis=2, concat_axis=3, tiled=True)  89.5 us
    all_gather x1, waiting for transfers between devices, local(): lax.all_gather(relaid_in, 'dp', axis=3, tiled=True)  68.2 us
    all_to_all x1, blocking collectives, local(): lax.all_to_all(lax.all_to_all(sectioned_down, 'dp', split_axis=2, concat_...  66 us
    all_to_all x1, blocking collectives, local(): lax.all_to_all(sectioned_down, 'dp', split_axis=2, concat_axis=3, tiled=T...  63 us
    all_to_all x1, blocking collectives, local(): lax.all_to_all(summed.reshape(experts, capacity, model_width), 'expert',...  20 us
    all_to_all x1, waiting for transfers between devices, exchange_gather(): blocks = lax.all_to_all(blocks, name, split_axis=0, concat_axis=0)  18.4 us
  transfers between devices with their start and end apart: 6, of which 5 were waited for; matrix products, arithmetic and copies ran while one was open for 6% of the time, Pallas kernels for 0%

profile of v1, /device:TPU:8, one launch (start us, length us, event | category | flops | bytes accessed | tf_op | source)
XLA Modules:
  0.0 660.6 jit_solution(4340669352122984994)
XLA Ops:
  6.5 0.0 copy-start
  6.5 0.8 multiply_add_fusion
  7.4 0.9 convert_reduce_fusion
  8.3 1.2 convolution_convert_fusion.1
  9.5 0.9 reshape.62
  10.4 8.5 %all-to-all-start = ((bf16[8,4,6144]{2,1,0:T(4,128)(2,1)}), bf16[8,4,6144]{2,1,0:T(4,128)(2,1)S(1)}, u32[]{:S(2)}, u32[]{:S(2)}) async-start(bf16[8,4,6144]{2,1,0:T(4,128)(2,1)} %reshape.62), calls=%async_computation | async-start | bytes 786432 | tf_op jit(solution)/shard_map/all_to_all | solution.py:44
  18.8 0.9 select_reduce_fusion.1
  19.7 6.4 gather_fusion
  26.1 3.5 broadcast_select_fusion
  29.6 3.1 copy.24
  32.6 0.9 all-to-all-done
  33.5 6.3 all-to-all-start.1
  39.8 0.0 all-gather.3.cloned.1.call-start
  39.9 0.8 reshape.63
  40.7 0.0 all-gather.3.cloned.1.call-update
  40.8 0.0 all-gather.5.cloned.1.call-start
  40.8 89.5 %all-to-all-done.1 = bf16[8,2,2,16,6144]{4,3,1,0,2:T(8,128)(2,1)} async-done(((bf16[8,2,2,16,6144]{4,3,1,0,2:T(8,128)(2,1)}), bf16[8,2,2,16,6144]{4,3,1,0,2:T(8,128)(2,1)}, u32[]{:S(2)}, u32[]{:S(2)}) %all-to-all-start.1) | async-done | bytes 6291488 | tf_op jit(solution)/shard_map/all_to_all | solution.py:58
  130.3 3.5 copy.25
  133.8 145.9 %all_to_all.66 = bf16[8,2,1,32,6144]{4,3,1,2,0:T(8,128)(2,1)S(1)} all-to-all(bf16[8,2,1,32,6144]{4,3,1,2,0:T(8,128)(2,1)S(1)} %bitcast.36), channel_id=1, replica_groups=mesh['dp'=2,'expert'=8,'shard'=16] {'expert'}, dimensions={0} | all-to-all | bytes 12582912 | tf_op jit(solution)/shard_map/all_to_all | solution.py:57
  279.7 3.1 copy.27
  282.8 0.0 all-gather.5.cloned.1.call-update
  282.8 0.0 copy-done
  282.8 2.4 gather_fusion.1
  285.2 2.3 bitcast_select_fusion
  287.5 0.3 copy.28
  287.8 63.0 %all_to_all.67 = bf16[8,1,2,16,6144]{4,3,0,1,2:T(8,128)(2,1)S(1)} all-to-all(bf16[8,1,2,16,6144]{4,3,0,1,2:T(8,128)(2,1)S(1)} %copy.28), channel_id=1, replica_groups=mesh['dp'=2,'expert'=8,'shard'=16] {'dp'}, dimensions={2} | all-to-all | bytes 6291456 | tf_op jit(solution)/shard_map/all_to_all | solution.py:65
  350.8 0.3 copy.29
  351.2 66.0 %all_to_all.68 = bf16[8,1,1,32,6144]{4,3,2,1,0:T(8,128)(2,1)S(1)} all-to-all(bf16[8,1,1,32,6144]{4,3,2,1,0:T(8,128)(2,1)S(1)} %bitcast.38), channel_id=1, replica_groups=mesh['dp'=2,'expert'=8,'shard'=16] {'expert'}, dimensions={0} | all-to-all | bytes 6291456 | tf_op jit(solution)/shard_map/all_to_all | solution.py:64
  417.2 3.2 pad_maximum_fusion
  420.4 6.3 all-to-all-start.5
  426.8 0.0 reduce-scatter.2.cloned.1.call-start
  426.8 0.0 all-gather.3.cloned.1.call-done
  426.8 68.2 %all-gather.5.cloned.1.call-done = bf16[1,2,1,512,6144]{4,3,1,2,0:T(8,128)(2,1)} async-done(((bf16[1,2,1,256,6144]{4,3,1,2,0:T(8,128)(2,1)}), bf16[1,2,1,512,6144]{4,3,1,2,0:T(8,128)(2,1)}) %all-gather.5.cloned.1.call-update) | async-done | bytes 12582928 | tf_op jit(solution)/shard_map/all_gather | solution.py:73
  495.0 12.5 %fusion = f32[512,2,512]{2,0,1:T(8,128)} fusion(bf16[1,2,1,512,6144]{4,3,1,2,0:T(8,128)(2,1)} %all-gather.5.cloned.1.call-done, bf16[512,6144]{1,0:T(8,128)(2,1)} %all-gather.3.cloned.1.call-done), kind=kOutput, calls=%fused_computation.2 | convolution fusion | flops 6442450944 | bytes 20971520 | tf_op jit(solution)/shard_map/rd,gud->rgu/dot_general | solution.py:21
  507.5 18.4 %all-to-all-done.5 = bf16[2,1,1,1,256,6144]{5,4,3,2,1,0:T(8,128)(2,1)} async-done(((bf16[2,1,1,1,256,6144]{5,4,3,2,1,0:T(8,128)(2,1)}), bf16[2,1,1,1,256,6144]{5,4,3,2,1,0:T(8,128)(2,1)}, u32[]{:S(2)}, u32[]{:S(2)}) %all-to-all-start.5) | async-done | bytes 6291488 | tf_op jit(solution)/shard_map/all_to_all | solution.py:10
  525.9 0.0 copy-start.1
  525.9 9.7 %convolution_convert_fusion = bf16[512,6144]{1,0:T(8,128)(2,1)} fusion(bf16[512,6144]{1,0:T(8,128)(2,1)} %bitcast.16, f32[512,2,512]{2,0,1:T(8,128)} %fusion), kind=kOutput, calls=%fused_computation.4 | convolution fusion | flops 3225944064 | bytes 14680064 | tf_op jit(solution)/shard_map/dot_general | solution.py:80
  535.6 0.0 reduce-scatter.2.cloned.1.call-update
  535.6 95.3 %reduce-scatter.2.cloned.1.call-done = bf16[32,6144]{1,0:T(8,128)(2,1)} async-done(((bf16[512,6144]{1,0:T(8,128)(2,1)}), bf16[32,6144]{1,0:T(8,128)(2,1)}) %reduce-scatter.2.cloned.1.call-update) | async-done | bytes 393232 | tf_op jit(solution)/shard_map/reduce_scatter | solution.py:79
  630.9 1.1 reshape.67
  632.0 20.0 %all_to_all.69 = bf16[8,4,6144]{2,1,0:T(4,128)(2,1)} all-to-all(bf16[8,4,6144]{2,1,0:T(4,128)(2,1)S(1)} %reshape.67), channel_id=1, replica_groups=mesh['dp'=2,'expert'=8,'shard'=16] {'expert'}, dimensions={0} | all-to-all | bytes 786432 | tf_op jit(solution)/shard_map/all_to_all | solution.py:87
  652.0 1.1 reshape.68
  653.1 0.9 convolution_convert_fusion.2
  654.0 0.0 copy-done.1
  (3 shorter events, 0.0 us)
Async XLA Ops:
  6.5 276.3 %copy-start = (bf16[8,32,6144]{2,1,0:T(8,128)(2,1)S(1)}, bf16[8,32,6144]{2,1,0:T(8,128)(2,1)}, u32[]{:S(2)}) copy-start(bf16[8,32,6144]{2,1,0:T(8,128)(2,1)} %param.10) | copy-start | bytes 9437188
  10.4 23.2 %all-to-all-start = ((bf16[8,4,6144]{2,1,0:T(4,128)(2,1)}), bf16[8,4,6144]{2,1,0:T(4,128)(2,1)S(1)}, u32[]{:S(2)}, u32[]{:S(2)}) async-start(bf16[8,4,6144]{2,1,0:T(4,128)(2,1)} %reshape.62), calls=%async_computation | async-start | bytes 786432 | tf_op jit(solution)/shard_map/all_to_all | solution.py:44
  33.5 96.8 %all-to-all-start.1 = ((bf16[8,2,2,16,6144]{4,3,1,0,2:T(8,128)(2,1)}), bf16[8,2,2,16,6144]{4,3,1,0,2:T(8,128)(2,1)}, u32[]{:S(2)}, u32[]{:S(2)}) async-start(bf16[8,2,2,16,6144]{4,3,1,0,2:T(8,128)(2,1)} %copy.24), calls=%async_computation.1 | async-start | bytes 12582912 | tf_op jit(solution)/shard_map/all_to_all | solution.py:58
  39.8 387.0 %all-gather.3.cloned.1.call-start = ((), (), s32[]{:S(2)}) async-start(), calls=%async_computation.8 | async-start | bytes 6684672 | tf_op jit(solution)/shard_map/all_gather | solution.py:78
  40.8 454.3 %all-gather.5.cloned.1.call-start = ((), (), s32[]{:S(2)}) async-start(), calls=%async_computation.9 | async-start | bytes 18874368 | tf_op jit(solution)/shard_map/all_gather | solution.py:73
  420.4 105.4 %all-to-all-start.5 = ((bf16[2,1,1,1,256,6144]{5,4,3,2,1,0:T(8,128)(2,1)}), bf16[2,1,1,1,256,6144]{5,4,3,2,1,0:T(8,128)(2,1)}, u32[]{:S(2)}, u32[]{:S(2)}) async-start(bf16[2,1,1,1,256,6144]{5,4,3,2,1,0:T(8,128)(2,1)} %pad_maximum_fusion), calls=%async_computation.5 | async-start | bytes 12582912 | tf_op jit(solution)/shard_map/all_to_all | solution.py:10
  426.8 204.1 %reduce-scatter.2.cloned.1.call-start = ((), (), s32[]{:S(2)}) async-start(), calls=%async_computation.10 | async-start | bytes 6684672 | tf_op jit(solution)/shard_map/reduce_scatter | solution.py:79
  525.9 128.2 %copy-start.1 = (bf16[8,32,6144]{2,1,0:T(8,128)(2,1)S(1)}, bf16[8,32,6144]{2,1,0:T(8,128)(2,1)}, u32[]{:S(2)}) copy-start(bf16[8,32,6144]{2,1,0:T(8,128)(2,1)} %param.10) | copy-start | bytes 9437188
Sparse Core Ops, SparseCore 0:
  43.4 90.1 all-gather.2
  282.9 212.0 all-gather.4
  535.7 95.1 reduce-scatter.1
